TPU v7x, 32 devices: a whole 2x2x4 slice. The times are simulated.
32 devices in a mesh: ctx: 4 (over z), head: 8 (over y, x, core).
Axes of the slice: x: 2, y: 2, z: 4, core: 2. Of those that a mesh axis runs over, the one named last changes fastest.
Arguments:
- layer_input: bfloat16 [1024, 4096], P(('ctx', 'head')), may hold values from -6 to 6
- w_query: bfloat16 [4096, 4096], P('ctx', 'head'), may hold values from -0.09375 to 0.09375
- w_key: bfloat16 [4096, 4096], P('ctx', 'head'), may hold values from -0.09375 to 0.09375
- w_value: bfloat16 [4096, 4096], P('ctx', 'head'), may hold values from -0.09375 to 0.09375
- w_out: bfloat16 [4096, 4096], P('head'), may hold values from -0.09375 to 0.09375
- log_decay: float32 [32, 1024], P('head', 'ctx'), may hold values from -2 to 0
- level_gain: float32 [32, 10], P('head'), may hold values from 0.5 to 2
- level_mask: int32 [8, 10], P('ctx'), may hold values 0 or 1
Outputs:
- layer_out: bfloat16 [1024, 4096], P(('ctx', 'head'))
All inputs are finite; a program needn't handle non-finite values. No bound on the sum of `level_mask` on one device may be relied on, other than what follows from the above.
Results may differ from a plain program's by a relative error of at most 0.023.
Values may be sent and summed in bfloat16 or wider, within the bound.
A program may use at most 64 MiB of HBM per device.

v0:
```python
import jax
import jax.numpy as jnp
from jax import lax
from jax.sharding import PartitionSpec as P

HEAD_DIM = 128
BLOCK = 128


def swapped(value, axis, stride):
    mask = 2**stride
    pairs = [(source, source ^ mask) for source in range(lax.axis_size(axis))]
    return lax.ppermute(value, axis, pairs)


def levels_of(first, second, count):
    mixed = jnp.bitwise_xor(first, second)
    result = jnp.zeros(mixed.shape, jnp.int32)
    for level_bit in range(count):
        result = result + (mixed >= 2**level_bit).astype(jnp.int32)
    return result


def unit_rows(block):
    floated = block.astype(jnp.float32)
    return (floated / jnp.sqrt(jnp.sum(floated * floated, axis=-1, keepdims=True) + 1e-06)).astype(
        jnp.bfloat16
    )


def on_device(layer_input, w_query, w_key, w_value, w_out, log_decay, level_gain, level_mask):
    full_query, full_key, full_value = (
        lax.all_gather(w_query, "ctx", axis=0, tiled=True),
        lax.all_gather(w_key, "ctx", axis=0, tiled=True),
        lax.all_gather(w_value, "ctx", axis=0, tiled=True),
    )
    piece = lax.all_gather(layer_input, "head", axis=0, tiled=True)
    outputs = [
        jnp.dot(piece, weight, preferred_element_type=jnp.float32).astype(jnp.bfloat16)
        for weight in (full_query, full_key, full_value)
    ]
    joined = jnp.concatenate(outputs, axis=1)
    width = full_query.shape[1]
    local_heads = width // HEAD_DIM
    span = joined.shape[0]
    query_unit = unit_rows(joined[:, :width].reshape(span, local_heads, HEAD_DIM))
    key_unit = unit_rows(joined[:, width : 2 * width].reshape(span, local_heads, HEAD_DIM))
    values = joined[:, 2 * width :].reshape(span, local_heads, HEAD_DIM)
    cum = jnp.cumsum(log_decay, axis=1)
    span_total = cum[:, -1]
    level_count = level_gain.shape[1]
    per_span = span // BLOCK
    ctx_index = lax.axis_index("ctx")
    blocks = ctx_index * per_span + jnp.arange(per_span, dtype=jnp.int32)
    level_range = jnp.arange(level_count, dtype=jnp.int32)
    near_levels = levels_of(blocks[:, None], blocks[None, :], level_count)
    near_onehot = (near_levels[..., None] == level_range).astype(jnp.float32)
    block_weight = level_mask.astype(jnp.float32)[:, None, :] * level_gain[None, :, :]
    near_block = jnp.einsum("bhl,bel->hbe", block_weight, near_onehot)
    scores = jnp.einsum("thd,shd->hts", query_unit, key_unit, preferred_element_type=jnp.float32)
    position = jnp.arange(span, dtype=jnp.int32)
    causal = position[:, None] >= position[None, :]
    spread = cum[:, :, None] - cum[:, None, :]
    decay_factor = jnp.where(causal, jnp.exp(jnp.where(causal, spread, 0.0)), 0.0)
    shaped = (scores * decay_factor).reshape(local_heads, per_span, BLOCK, per_span, BLOCK)
    near_weight = (
        (shaped * near_block[:, :, None, :, None])
        .reshape(local_heads, span, span)
        .astype(jnp.bfloat16)
    )
    near_out = jnp.einsum("hts,shd->thd", near_weight, values, preferred_element_type=jnp.float32)
    decayed_key = (
        key_unit.astype(jnp.float32) * jnp.exp(span_total[None, :] - cum.T)[:, :, None]
    ).astype(jnp.bfloat16)
    span_state = jnp.einsum("thd,the->hde", decayed_key, values, preferred_element_type=jnp.float32)
    bit_count = lax.axis_size("ctx").bit_length() - 1
    bit_range = jnp.arange(bit_count, dtype=jnp.int32)
    powers = jnp.left_shift(jnp.ones_like(bit_range), bit_range)
    group_total, group_state = (span_total, span_state)
    before = jnp.zeros_like(span_total)
    collected = []
    for bit_index in range(bit_count):
        other_total, other_state = (
            swapped(group_total.astype(jnp.bfloat16), "ctx", bit_index).astype(group_total.dtype),
            swapped(group_state.astype(jnp.bfloat16), "ctx", bit_index).astype(group_state.dtype),
        )
        upper = jnp.bitwise_and(jnp.right_shift(ctx_index, bit_index), 1) == 1
        collected.append(jnp.where(upper, jnp.exp(before)[:, None, None] * other_state, 0.0))
        lower_total = jnp.where(upper, other_total, group_total)
        higher_total = jnp.where(upper, group_total, other_total)
        lower_state = jnp.where(upper, other_state, group_state)
        higher_state = jnp.where(upper, group_state, other_state)
        group_state = jnp.exp(higher_total)[:, None, None] * lower_state + higher_state
        group_total = lower_total + higher_total
        before = before + jnp.where(upper, other_total, 0.0)
    carried = jnp.stack(collected, axis=0)
    partner = jnp.bitwise_xor(ctx_index, powers)
    far_levels = levels_of(blocks[:, None], (partner * per_span)[None, :], level_count)
    far_onehot = (far_levels[..., None] == level_range).astype(jnp.float32)
    far_block = jnp.einsum("bhl,bml->bhm", block_weight, far_onehot)
    far_tokens = jnp.repeat(far_block, BLOCK, axis=0)
    scaled = query_unit.astype(jnp.float32) * jnp.exp(cum.T)[:, :, None]
    reached = jnp.einsum("thd,mhde->thme", scaled, carried, precision=lax.Precision.HIGHEST)
    far_out = jnp.einsum("thme,thm->the", reached, far_tokens, precision=lax.Precision.HIGHEST)
    heads_out = (near_out + far_out).astype(jnp.bfloat16).reshape(span, width)
    return lax.psum_scatter(
        jnp.dot(heads_out, w_out, preferred_element_type=jnp.float32).astype(jnp.bfloat16),
        "head",
        scatter_dimension=0,
        tiled=True,
    )


def solution(mesh):
    in_specs = (
        P(("ctx", "head"), None),
        P("ctx", "head"),
        P("ctx", "head"),
        P("ctx", "head"),
        P("head", None),
        P("head", "ctx"),
        P("head", None),
        P("ctx", None),
    )
    out_specs = P(("ctx", "head"), None)
    return jax.shard_map(
        on_device, mesh=mesh, in_specs=in_specs, out_specs=out_specs, check_vma=False
    )
```

profile of v0, /device:TPU:0, one launch (start us, length us, event | category | flops | bytes accessed | tf_op | source)
XLA Modules:
  0.0 354.7 jit_solution(5729758578422168812)
XLA Ops:
  6.5 0.7 all-gather.5.cloned.1.call-update
  7.3 0.7 all-gather.9.cloned.1.call-update
  8.1 0.7 all-gather.11.cloned.1.call-update
  8.8 0.5 all-gather.7.cloned.1.call-update
  9.4 0.7 reshape.199
  10.1 1.2 reduce-window.6
  11.3 0.1 slice.12
  11.3 0.1 copy.19
  11.5 0.1 copy.20
  11.6 0.1 add_bitcast_fusion
  11.7 0.1 slice.13
  11.7 0.1 copy.39
  11.8 3.1 collective-permute-start.1
  14.9 0.7 convert_element_type.227
  15.6 0.1 fusion.73
  15.7 0.9 convolution_bitcast_fusion.2
  16.6 0.1 copy.21
  16.7 0.1 copy.24
  16.9 0.1 copy.27
  17.0 0.9 fusion.33
  17.9 0.1 broadcast_in_dim.27
  18.0 0.2 copy.40
  18.2 0.3 mul.82
  18.5 0.8 mul.83
  19.4 20.3 %all-gather.5.cloned.1.call-done = bf16[256,4096]{1,0:T(8,128)(2,1)} async-done(((bf16[32,4096]{1,0:T(8,128)(2,1)}), bf16[256,4096]{1,0:T(8,128)(2,1)}) %all-gather.5.cloned.1.call-update) | async-done | bytes 2097168 | tf_op jit(solution)/shard_map/all_gather | solution.py:37
  39.8 82.3 %all-gather.9.cloned.1.call-done = bf16[4096,512]{1,0:T(8,128)(2,1)} async-done(((bf16[1024,512]{1,0:T(8,128)(2,1)}), bf16[4096,512]{1,0:T(8,128)(2,1)}) %all-gather.9.cloned.1.call-update) | async-done | bytes 4194320 | tf_op jit(solution)/shard_map/all_gather | solution.py:33
  122.1 4.1 %fusion.7 = f32[256,512]{1,0:T(8,128)S(1)} fusion(bf16[256,4096]{1,0:T(8,128)(2,1)} %all-gather.5.cloned.1.call-done, bf16[4096,512]{1,0:T(8,128)(2,1)} %all-gather.9.cloned.1.call-done), kind=kOutput, calls=%fused_computation.13 | convolution fusion | flops 1074003968 | bytes 6815744 | tf_op jit(solution)/shard_map/dot_general | solution.py:39
  126.2 0.2 reshape.203
  126.3 76.6 %all-gather.11.cloned.1.call-done = bf16[4096,512]{1,0:T(8,128)(2,1)} async-done(((bf16[1024,512]{1,0:T(8,128)(2,1)}), bf16[4096,512]{1,0:T(8,128)(2,1)}) %all-gather.11.cloned.1.call-update) | async-done | bytes 4194320 | tf_op jit(solution)/shard_map/all_gather | solution.py:34
  202.9 4.1 %fusion.6 = f32[256,512]{1,0:T(8,128)S(1)} fusion(bf16[256,4096]{1,0:T(8,128)(2,1)} %all-gather.5.cloned.1.call-done, bf16[4096,512]{1,0:T(8,128)(2,1)} %all-gather.11.cloned.1.call-done), kind=kOutput, calls=%fused_computation.11 | convolution fusion | flops 1074003968 | bytes 6815744 | tf_op jit(solution)/shard_map/dot_general | solution.py:39
  207.0 0.2 reshape.204
  207.2 0.3 multiply_reduce_fusion
  207.5 0.3 multiply_reduce_fusion.1
  207.9 0.7 multiply_convert_fusion
  208.6 75.0 %all-gather.7.cloned.1.call-done = bf16[4096,512]{1,0:T(8,128)(2,1)} async-done(((bf16[1024,512]{1,0:T(8,128)(2,1)}), bf16[4096,512]{1,0:T(8,128)(2,1)}) %all-gather.7.cloned.1.call-update) | async-done | bytes 4194320 | tf_op jit(solution)/shard_map/all_gather | solution.py:35
  283.6 4.1 %fusion.8 = bf16[32,4,8,128]{3,2,1,0:T(8,128)(2,1)S(1)} fusion(bf16[256,4096]{1,0:T(8,128)(2,1)} %all-gather.5.cloned.1.call-done, bf16[4096,512]{1,0:T(8,128)(2,1)} %all-gather.7.cloned.1.call-done), kind=kOutput, calls=%fused_computation.15 | convolution fusion | flops 1073872896 | bytes 6553600 | tf_op jit(solution)/shard_map/dot_general | solution.py:39
  287.7 0.3 fusion.87
  288.0 0.1 collective-permute-start
  288.1 5.0 %collective-permute-done = bf16[4,128,128]{2,1,0:T(8,128)(2,1)S(1)} collective-permute-done((bf16[4,128,128]{2,1,0:T(8,128)(2,1)S(1)}, bf16[4,128,128]{2,1,0:T(8,128)(2,1)S(1)}, u32[]{:S(2)}, u32[]{:S(2)}) %collective-permute-start) | collective-permute-done | bytes 131104 | tf_op jit(solution)/shard_map/ppermute | solution.py:13
  293.1 0.1 fusion.19
  293.2 0.9 collective-permute-start.2
  294.2 0.7 multiply_bitcast_fusion
  294.9 6.4 %collective-permute-done.2 = bf16[4,128,128]{2,1,0:T(8,128)(2,1)S(1)} collective-permute-done((bf16[4,128,128]{2,1,0:T(8,128)(2,1)S(1)}, bf16[4,128,128]{2,1,0:T(8,128)(2,1)S(1)}, u32[]{:S(2)}, u32[]{:S(2)}) %collective-permute-start.2) | collective-permute-done | bytes 131104 | tf_op jit(solution)/shard_map/ppermute | solution.py:13
  301.2 0.1 select_bitcast_fusion
  301.3 1.1 fusion.3
  302.4 0.6 fusion.5
  303.0 4.8 %convolution_convert_fusion = bf16[256,4096]{1,0:T(8,128)(2,1)} fusion(bf16[256,512]{0,1:T(8,128)(2,1)S(1)} %bitcast.57, bf16[512,4096]{1,0:T(8,128)(2,1)} %param.12), kind=kOutput, calls=%fused_computation | convolution fusion | flops 1074790400 | bytes 6553600 | tf_op jit(solution)/shard_map/dot_general | solution.py:107
  307.9 40.3 %reduce-scatter.2.cloned.1.call-done = bf16[32,4096]{1,0:T(8,128)(2,1)} async-done(((bf16[256,4096]{1,0:T(8,128)(2,1)}), bf16[32,4096]{1,0:T(8,128)(2,1)}) %reduce-scatter.2.cloned.1.call-update) | async-done | bytes 262160 | tf_op jit(solution)/shard_map/reduce_scatter | solution.py:106
  (17 shorter events, 0.4 us)
Async XLA Ops:
  6.5 33.2 %all-gather.5.cloned.1.call-start = ((), (), s32[]{:S(2)}) async-start(), calls=%async_computation.1 | async-start | bytes 2359296 | tf_op jit(solution)/shard_map/all_gather | solution.py:37
  7.3 114.8 %all-gather.9.cloned.1.call-start = ((), (), s32[]{:S(2)}) async-start(), calls=%async_computation.3 | async-start | bytes 5242880 | tf_op jit(solution)/shard_map/all_gather | solution.py:33
  8.0 194.9 %all-gather.11.cloned.1.call-start = ((), (), s32[]{:S(2)}) async-start(), calls=%async_computation.4 | async-start | bytes 5242880 | tf_op jit(solution)/shard_map/all_gather | solution.py:34
  8.7 274.9 %all-gather.7.cloned.1.call-start = ((), (), s32[]{:S(2)}) async-start(), calls=%async_computation.2 | async-start | bytes 5242880 | tf_op jit(solution)/shard_map/all_gather | solution.py:35
  9.3 338.8 %reduce-scatter.2.cloned.1.call-start = ((), (), s32[]{:S(2)}) async-start(), calls=%async_computation.5 | async-start | bytes 2359296 | tf_op jit(solution)/shard_map/reduce_scatter | solution.py:106
  11.8 7.6 %collective-permute-start.1 = (bf16[4]{0:T(256)(128)(2,1)S(1)}, bf16[4]{0:T(256)(128)(2,1)S(1)}, u32[]{:S(2)}, u32[]{:S(2)}) collective-permute-start(bf16[4]{0:T(256)(128)(2,1)S(1)} %bitcast_convert_fusion), channel_id=1, source_target_pairs={{0,8},{8,0},{16,24},{24,16},{1,9},{9,1},{17,25},{25,17},{2,10},{10... | collective-permute-start | bytes 32 | tf_op jit(solution)/shard_map/ppermute | solution.py:13
  288.0 5.2 %collective-permute-start = (bf16[4,128,128]{2,1,0:T(8,128)(2,1)S(1)}, bf16[4,128,128]{2,1,0:T(8,128)(2,1)S(1)}, u32[]{:S(2)}, u32[]{:S(2)}) collective-permute-start(bf16[4,128,128]{2,1,0:T(8,128)(2,1)S(1)} %get-tuple-element.17), channel_id=1, source_target_pairs={{0,8},{8,0},{16,24},{24,16},{1,9},{9,1},{17,25},{25,17},{2,10},{10... | collective-permute-start | bytes 393224 | tf_op jit(solution)/shard_map/ppermute | solution.py:13
  293.2 8.0 %collective-permute-start.2 = (bf16[4,128,128]{2,1,0:T(8,128)(2,1)S(1)}, bf16[4,128,128]{2,1,0:T(8,128)(2,1)S(1)}, u32[]{:S(2)}, u32[]{:S(2)}) collective-permute-start(bf16[4,128,128]{2,1,0:T(8,128)(2,1)S(1)} %get-tuple-element.10), channel_id=1, source_target_pairs={{0,16},{8,24},{16,0},{24,8},{1,17},{9,25},{17,1},{25,9},{2,18},{10... | collective-permute-start | bytes 393224 | tf_op jit(solution)/shard_map/ppermute | solution.py:13
Sparse Core Ops, SparseCore 0:
  9.2 30.4 all-gather.4
  41.3 80.7 all-gather.8
  123.7 79.2 all-gather.10
  204.3 79.2 all-gather.6
  308.0 40.1 reduce-scatter.1
where the time goes:
time: 355 us
  waiting for transfers between devices  308 us (87%)
  matrix products  20.7 us (6%)
  between operations  13.3 us (4%)
  other arithmetic  4.58 us (1%)
  starting transfers between devices  4.23 us (1%)
    all_gather x1, waiting for transfers between devices, on_device(): lax.all_gather(w_query, 'ctx', axis=0, tiled=True)  82.3 us
    all_gather x1, waiting for transfers between devices, on_device(): lax.all_gather(w_key, 'ctx', axis=0, tiled=True)  76.6 us
    all_gather x1, waiting for transfers between devices, on_device(): lax.all_gather(w_value, 'ctx', axis=0, tiled=True)  75 us
    reduce_scatter x1, waiting for transfers between devices, on_device(): lax.psum_scatter(jnp.dot(heads_out, w_out, preferred_element_type=jnp.flo...  40.3 us
    all_gather x1, waiting for transfers between devices, on_device(): piece = lax.all_gather(layer_input, 'head', axis=0, tiled=True)  20.3 us
    dot_general x3, matrix products, on_device(): jnp.dot(piece, weight, preferred_element_type=jnp.float32)  12.2 us
    ppermute x3, waiting for transfers between devices, swapped(): return lax.ppermute(value, axis, pairs)  11.4 us
  transfers between devices with their start and end apart: 8, of which 7 were waited for; matrix products, arithmetic and copies ran while one was open for 5% of the time, Pallas kernels for 0%

commit v1 on v0

--- a/solution.py
+++ b/solution.py
@@ -5,6 +5,19 @@
 
 HEAD_DIM = 128
 BLOCK = 128
+
+
+def collect(x, axis, dim):
+    ways = lax.axis_size(axis)
+    up = [(d, (d + 1) % ways) for d in range(ways)]
+    down = [(d, (d - 1) % ways) for d in range(ways)]
+    earlier, later = ([x], [x])
+    for _ in range(ways // 2):
+        earlier.append(lax.ppermute(earlier[-1], axis, up))
+    for _ in range((ways - 1) // 2):
+        later.append(lax.ppermute(later[-1], axis, down))
+    line = jnp.concatenate([*earlier[::-1], *later[1:]], axis=dim)
+    return jnp.roll(line, (lax.axis_index(axis) - ways // 2) * x.shape[dim], axis=dim)
 
 
 def swapped(value, axis, stride):
@@ -32,7 +45,7 @@
     full_query, full_key, full_value = (
         lax.all_gather(w_query, "ctx", axis=0, tiled=True),
         lax.all_gather(w_key, "ctx", axis=0, tiled=True),
-        lax.all_gather(w_value, "ctx", axis=0, tiled=True),
+        collect(w_value, "ctx", 0),
     )
     piece = lax.all_gather(layer_input, "head", axis=0, tiled=True)
     outputs = [

time: 355 us -> 299 us (0.84)
  waiting for transfers between devices: 308 us -> 234 us
  local copies, waits for them, and re-layouts: 3.36 us -> 19.4 us
    all_gather x1 -> x0, waiting for transfers between devices: 75 us -> none  [on_device(): lax.all_gather(w_value, 'ctx', axis=0, tiled=True)]
    ppermute x0 -> x3, waiting for transfers between devices: none -> 53.4 us  [the longest x2 53.4 us: collect(): earlier.append(lax.ppermute(earlier[-1], axis, up))]
    all_gather x1, waiting for transfers between devices: 76.6 us -> 23.8 us  [on_device(): lax.all_gather(w_key, 'ctx', axis=0, tiled=True)]
    ppermute x3, waiting for transfers between devices: 11.4 us -> 37.5 us  [swapped(): return lax.ppermute(value, axis, pairs)]
    all_gather x1, waiting for transfers between devices: 20.3 us -> 0.01 us  [on_device(): piece = lax.all_gather(layer_input, 'head', axis=0, tiled=True)]
    unnamed x3 -> x14, local copies, waits for them, and re-layouts: 0.3 us -> 11.3 us
    all_gather x1, waiting for transfers between devices: 82.3 us -> 75.7 us  [on_device(): lax.all_gather(w_query, 'ctx', axis=0, tiled=True)]
    ppermute x0 -> x3, starting transfers between devices: none -> 5.2 us  [the longest x2 3.11 us: collect(): earlier.append(lax.ppermute(earlier[-1], axis, up))]
  transfers between devices with their start and end apart: 8 -> 10, of which waited for: 7 -> 7; matrix products, arithmetic and copies ran while one was open for 5% -> 13% of each run, Pallas kernels for 0% -> 0%
where the time goes in v1:
time: 299 us; the launch traced here: 298 us
  waiting for transfers between devices  234 us (78%)
  matrix products  20.8 us (7%)
  local copies, waits for them, and re-layouts  19.4 us (6%)
  between operations  13.3 us (4%)
  starting transfers between devices  6.36 us (2%)
  other arithmetic  4.58 us (2%)
    all_gather x1, waiting for transfers between devices, on_device(): lax.all_gather(w_query, 'ctx', axis=0, tiled=True)  75.7 us
    ppermute x2, waiting for transfers between devices, collect(): earlier.append(lax.ppermute(earlier[-1], axis, up))  53.4 us
    reduce_scatter x1, waiting for transfers between devices, on_device(): lax.psum_scatter(jnp.dot(heads_out, w_out, preferred_element_type=jnp.flo...  41.5 us
    ppermute x3, waiting for transfers between devices, swapped(): return lax.ppermute(value, axis, pairs)  37.5 us
    all_gather x1, waiting for transfers between devices, on_device(): lax.all_gather(w_key, 'ctx', axis=0, tiled=True)  23.8 us
    dot_general x3, matrix products, on_device(): jnp.dot(piece, weight, preferred_element_type=jnp.float32)  12.3 us
    unnamed x14, local copies, waits for them, and re-layouts  11.3 us
  transfers between devices with their start and end apart: 10, of which 7 were waited for; matrix products, arithmetic and copies ran while one was open for 13% of the time, Pallas kernels for 0%

profile of v1, /device:TPU:0, one launch (start us, length us, event | category | flops | bytes accessed | tf_op | source)
XLA Modules:
  0.0 298.5 jit_solution(7463512729468975048)
XLA Ops:
  6.5 0.7 all-gather.4.cloned.1.call-update
  7.3 0.7 all-gather.8.cloned.1.call-update
  8.1 0.7 all-gather.6.cloned.1.call-update
  8.8 3.1 %collective-permute-start = (bf16[1024,512]{1,0:T(8,128)(2,1)}, bf16[1024,512]{1,0:T(8,128)(2,1)S(1)}, u32[]{:S(2)}, u32[]{:S(2)}) collective-permute-start(bf16[1024,512]{1,0:T(8,128)(2,1)} %param.11), channel_id=1, source_target_pairs={{0,8},{8,16},{16,24},{24,0},{1,9},{9,17},{17,25},{25,1},{2,10},{10... | collective-permute-start | bytes 3145736 | tf_op jit(solution)/shard_map/ppermute | solution.py:16
  11.9 2.1 collective-permute-start.2
  14.0 0.7 reshape.199
  14.7 1.2 reduce-window.6
  16.0 0.1 copy.18
  16.5 21.7 %collective-permute-done = bf16[1024,512]{1,0:T(8,128)(2,1)S(1)} collective-permute-done((bf16[1024,512]{1,0:T(8,128)(2,1)}, bf16[1024,512]{1,0:T(8,128)(2,1)S(1)}, u32[]{:S(2)}, u32[]{:S(2)}) %collective-permute-start) | collective-permute-done | bytes 1048608 | tf_op jit(solution)/shard_map/ppermute | solution.py:16
  38.3 0.7 convert_element_type.231
  39.0 0.9 fusion.33
  39.9 0.1 copy.22
  40.1 0.9 broadcast_in_dim.27
  40.9 1.3 copy.39
  42.2 0.1 copy.25
  42.4 0.9 convolution_bitcast_fusion.2
  43.3 0.1 copy.20
  43.4 1.3 mul.86
  44.7 3.0 %mul.87 = f32[4,256,256]{2,1,0:T(8,128)} reshape(f32[4,2,128,2,128]{4,3,2,1,0:T(2,128)} %mul.86) | data formatting | bytes 2097152 | tf_op jit(solution)/shard_map/mul | solution.py:80
  47.8 31.9 %collective-permute-done.4 = bf16[4]{0:T(256)(128)(2,1)S(1)} collective-permute-done((bf16[4]{0:T(256)(128)(2,1)S(1)}, bf16[4]{0:T(256)(128)(2,1)S(1)}, u32[]{:S(2)}, u32[]{:S(2)}) %collective-permute-start.4) | collective-permute-done | bytes 40 | tf_op jit(solution)/shard_map/ppermute | solution.py:26
  79.6 31.7 %collective-permute-done.1 = bf16[1024,512]{1,0:T(8,128)(2,1)} collective-permute-done((bf16[1024,512]{1,0:T(8,128)(2,1)S(1)}, bf16[1024,512]{1,0:T(8,128)(2,1)}, u32[]{:S(2)}, u32[]{:S(2)}) %collective-permute-start.1) | collective-permute-done | bytes 1048608 | tf_op jit(solution)/shard_map/ppermute | solution.py:16
  111.3 2.3 constant_dynamic-update-slice_fusion.7
  113.6 1.1 constant_dynamic-update-slice_fusion.6
  114.7 1.1 constant_dynamic-update-slice_fusion.5
  115.8 1.1 constant_dynamic-update-slice_fusion.4
  116.8 2.3 constant_dynamic-update-slice_fusion.3
  119.1 1.1 constant_dynamic-update-slice_fusion.2
  120.1 1.1 constant_dynamic-update-slice_fusion.1
  121.2 1.1 constant_dynamic-update-slice_fusion
  122.3 4.2 %fusion.8 = bf16[512,256]{1,0:T(8,128)(2,1)S(1)} fusion(bf16[256,4096]{1,0:T(8,128)(2,1)} %all-gather.4.cloned.1.call-done, bf16[8192,512]{1,0:T(8,128)(2,1)} %constant_dynamic-update-slice_fusion, s32[]{:T(128)S(6)} %select_n.59), kind=kOutput, calls=%fused_computation.12 | convolution fusion | flops 1073872896 | bytes 6553604 | tf_op jit(solution)/shard_map/dot_general | solution.py:52
  126.5 23.8 %all-gather.8.cloned.1.call-done = bf16[4096,512]{1,0:T(8,128)(2,1)} async-done(((bf16[1024,512]{1,0:T(8,128)(2,1)}), bf16[4096,512]{1,0:T(8,128)(2,1)}) %all-gather.8.cloned.1.call-update) | async-done | bytes 4194320 | tf_op jit(solution)/shard_map/all_gather | solution.py:47
  150.3 4.1 %fusion.11 = f32[256,512]{1,0:T(8,128)S(1)} fusion(bf16[256,4096]{1,0:T(8,128)(2,1)} %all-gather.4.cloned.1.call-done, bf16[4096,512]{1,0:T(8,128)(2,1)} %all-gather.8.cloned.1.call-done), kind=kOutput, calls=%fused_computation.14 | convolution fusion | flops 1074003968 | bytes 6815744 | tf_op jit(solution)/shard_map/dot_general | solution.py:52
  154.3 0.2 reshape.204
  154.5 0.3 multiply_reduce_fusion
  154.9 0.7 multiply_convert_fusion
  155.6 0.3 fusion.88
  156.0 75.7 %all-gather.6.cloned.1.call-done = bf16[4096,512]{1,0:T(8,128)(2,1)} async-done(((bf16[1024,512]{1,0:T(8,128)(2,1)}), bf16[4096,512]{1,0:T(8,128)(2,1)}) %all-gather.6.cloned.1.call-update) | async-done | bytes 4194320 | tf_op jit(solution)/shard_map/all_gather | solution.py:46
  231.7 4.1 %fusion.12 = f32[256,512]{1,0:T(8,128)S(1)} fusion(bf16[256,4096]{1,0:T(8,128)(2,1)} %all-gather.4.cloned.1.call-done, bf16[4096,512]{1,0:T(8,128)(2,1)} %all-gather.6.cloned.1.call-done), kind=kOutput, calls=%fused_computation.16 | convolution fusion | flops 1074003968 | bytes 6815744 | tf_op jit(solution)/shard_map/dot_general | solution.py:52
  235.8 0.2 reshape.203
  236.0 0.3 multiply_reduce_fusion.1
  236.4 0.1 fusion.23
  236.5 1.0 collective-permute-start.5
  237.5 0.7 multiply_bitcast_fusion
  238.2 5.6 %collective-permute-done.5 = bf16[4,128,128]{2,1,0:T(8,128)(2,1)S(1)} collective-permute-done((bf16[4,128,128]{2,1,0:T(8,128)(2,1)S(1)}, bf16[4,128,128]{2,1,0:T(8,128)(2,1)S(1)}, u32[]{:S(2)}, u32[]{:S(2)}) %collective-permute-start.5) | collective-permute-done | bytes 131104 | tf_op jit(solution)/shard_map/ppermute | solution.py:26
  243.9 1.1 fusion.5
  245.0 0.6 fusion.7
  245.6 4.8 %convolution_convert_fusion = bf16[256,4096]{1,0:T(8,128)(2,1)} fusion(bf16[256,512]{0,1:T(8,128)(2,1)S(1)} %bitcast.54, bf16[512,4096]{1,0:T(8,128)(2,1)} %param.12), kind=kOutput, calls=%fused_computation | convolution fusion | flops 1074790400 | bytes 6553600 | tf_op jit(solution)/shard_map/dot_general | solution.py:120
  250.4 41.5 %reduce-scatter.2.cloned.1.call-done = bf16[32,4096]{1,0:T(8,128)(2,1)} async-done(((bf16[256,4096]{1,0:T(8,128)(2,1)}), bf16[32,4096]{1,0:T(8,128)(2,1)}) %reduce-scatter.2.cloned.1.call-update) | async-done | bytes 262160 | tf_op jit(solution)/shard_map/reduce_scatter | solution.py:119
  (32 shorter events, 1.0 us)
Async XLA Ops:
  6.5 115.8 %all-gather.4.cloned.1.call-start = ((), (), s32[]{:S(2)}) async-start(), calls=%async_computation.1 | async-start | bytes 2359296 | tf_op jit(solution)/shard_map/all_gather | solution.py:50
  7.3 143.0 %all-gather.8.cloned.1.call-start = ((), (), s32[]{:S(2)}) async-start(), calls=%async_computation.3 | async-start | bytes 5242880 | tf_op jit(solution)/shard_map/all_gather | solution.py:47
  8.0 223.7 %all-gather.6.cloned.1.call-start = ((), (), s32[]{:S(2)}) async-start(), calls=%async_computation.2 | async-start | bytes 5242880 | tf_op jit(solution)/shard_map/all_gather | solution.py:46
  8.7 283.2 %reduce-scatter.2.cloned.1.call-start = ((), (), s32[]{:S(2)}) async-start(), calls=%async_computation.4 | async-start | bytes 2359296 | tf_op jit(solution)/shard_map/reduce_scatter | solution.py:119
  8.8 29.4 %collective-permute-start = (bf16[1024,512]{1,0:T(8,128)(2,1)}, bf16[1024,512]{1,0:T(8,128)(2,1)S(1)}, u32[]{:S(2)}, u32[]{:S(2)}) collective-permute-start(bf16[1024,512]{1,0:T(8,128)(2,1)} %param.11), channel_id=1, source_target_pairs={{0,8},{8,16},{16,24},{24,0},{1,9},{9,17},{17,25},{25,1},{2,10},{10... | collective-permute-start | bytes 3145736 | tf_op jit(solution)/shard_map/ppermute | solution.py:16
  11.9 103.9 %collective-permute-start.2 = (bf16[1024,512]{1,0:T(8,128)(2,1)}, bf16[1024,512]{1,0:T(8,128)(2,1)S(1)}, u32[]{:S(2)}, u32[]{:S(2)}) collective-permute-start(bf16[1024,512]{1,0:T(8,128)(2,1)} %param.11), channel_id=1, source_target_pairs={{0,24},{8,0},{16,8},{24,16},{1,25},{9,1},{17,9},{25,17},{2,26},{10... | collective-permute-start | bytes 3145736 | tf_op jit(solution)/shard_map/ppermute | solution.py:18
  16.5 63.2 %collective-permute-start.4 = (bf16[4]{0:T(256)(128)(2,1)S(1)}, bf16[4]{0:T(256)(128)(2,1)S(1)}, u32[]{:S(2)}, u32[]{:S(2)}) collective-permute-start(bf16[4]{0:T(256)(128)(2,1)S(1)} %bitcast_convert_fusion), channel_id=1, source_target_pairs={{0,8},{8,0},{16,24},{24,16},{1,9},{9,1},{17,25},{25,17},{2,10},{10... | collective-permute-start | bytes 32 | tf_op jit(solution)/shard_map/ppermute | solution.py:26
  38.2 73.1 %collective-permute-start.1 = (bf16[1024,512]{1,0:T(8,128)(2,1)S(1)}, bf16[1024,512]{1,0:T(8,128)(2,1)}, u32[]{:S(2)}, u32[]{:S(2)}) collective-permute-start(bf16[1024,512]{1,0:T(8,128)(2,1)S(1)} %collective-permute-done), channel_id=1, source_target_pairs={{0,8},{8,16},{16,24},{24,0},{1,9},{9,17},{17,25},{25,1},{2,10},{10... | collective-permute-start | bytes 3145736 | tf_op jit(solution)/shard_map/ppermute | solution.py:16
  40.9 73.8 %copy-start = (bf16[1024,512]{1,0:T(8,128)(2,1)S(1)}, bf16[1024,512]{1,0:T(8,128)(2,1)}, u32[]{:S(2)}) copy-start(bf16[1024,512]{1,0:T(8,128)(2,1)} %param.11) | copy-start | bytes 3145732
  155.9 80.5 %collective-permute-start.3 = (bf16[4,128,128]{2,1,0:T(8,128)(2,1)S(1)}, bf16[4,128,128]{2,1,0:T(8,128)(2,1)S(1)}, u32[]{:S(2)}, u32[]{:S(2)}) collective-permute-start(bf16[4,128,128]{2,1,0:T(8,128)(2,1)S(1)} %get-tuple-element.17), channel_id=1, source_target_pairs={{0,8},{8,0},{16,24},{24,16},{1,9},{9,1},{17,25},{25,17},{2,10},{10... | collective-permute-start | bytes 393224 | tf_op jit(solution)/shard_map/ppermute | solution.py:26
  235.8 9.2 %copy-start.1 = (f32[4,256,256]{2,1,0:T(8,128)S(1)}, f32[4,256,256]{2,1,0:T(8,128)}, u32[]{:S(2)}) copy-start(f32[4,256,256]{2,1,0:T(8,128)} %mul.87) | copy-start | bytes 3145732
  236.5 7.3 %collective-permute-start.5 = (bf16[4,128,128]{2,1,0:T(8,128)(2,1)S(1)}, bf16[4,128,128]{2,1,0:T(8,128)(2,1)S(1)}, u32[]{:S(2)}, u32[]{:S(2)}) collective-permute-start(bf16[4,128,128]{2,1,0:T(8,128)(2,1)S(1)} %get-tuple-element.10), channel_id=1, source_target_pairs={{0,16},{8,24},{16,0},{24,8},{1,17},{9,25},{17,1},{25,9},{2,18},{10... | collective-permute-start | bytes 393224 | tf_op jit(solution)/shard_map/ppermute | solution.py:26
Sparse Core Ops, SparseCore 0:
  9.2 30.4 all-gather.3
  41.3 108.8 all-gather.7
  151.8 79.8 all-gather.5
  250.6 41.3 reduce-scatter.1
